TPU v7x, 32 devices: a whole 2x2x4 slice. The times are simulated.
32 devices in a mesh: slab: 2 (over y), strip: 16 (over z, x, core).
Axes of the slice: x: 2, y: 2, z: 4, core: 2. Of those that a mesh axis runs over, the one named last changes fastest.
Arguments:
- volume: bfloat16 [8, 512, 1024], P('slab', 'strip'), may hold values from -1 to 1
- shear: int32 [2, 8], P(None, 'slab'), may hold values from -64 to 64, as said below
- probe: float32 [2, 128, 128], replicated, may hold values from -4 to 4
- positions: int32 [2, 16, 16, 2], P('slab', 'strip'), may hold values from -64 to 192, as said below
- measured: bfloat16 [2, 16, 16, 128, 128], P('slab', 'strip'), may hold values from 0.099609375 to 4
Outputs:
- volume_grad: bfloat16 [8, 512, 1024], P('slab', 'strip')
Inputs may be any that keep to these rules, and one draw needn't show every extreme that they name: shear[v, z] is the floor of s_v (2 ((z + r_v) mod 8) - 8) / 8 for integers s_v from -64 to 64 and r_v from 0 to 7. `positions`: row offsets (last index 0) lie from -64 to 192, column offsets (last index 1) from -64 to 64, so every patch lies within 64 pixels of its tile.
All inputs are finite; a program needn't handle non-finite values.
Results may differ from a plain program's by a relative error of at most 0.023.
Values may be sent and summed in bfloat16 or wider, within the bound.
A program may use at most 64 MiB of HBM per device.

v0:
```python
import functools
import math

import jax
import jax.numpy as jnp
import numpy as np
from jax import lax
from jax.experimental import pallas as pl
from jax.experimental.pallas import tpu as pltpu
from jax.sharding import PartitionSpec as P

TILE_W = 128
PATCH = 128
RIM = PATCH // 2
WIN = TILE_W + 2 * RIM
GRAD_SCALE = 0.125
MESH = pl.DeviceIdType.MESH
F32 = jnp.float32
BF16 = jnp.bfloat16


def dft_tables():
    index = np.arange(PATCH)
    angle = 2.0 * math.pi * ((index[:, None] * index[None, :]) % PATCH) / PATCH
    cosine = np.cos(angle) / math.sqrt(PATCH)
    sine = np.sin(angle) / math.sqrt(PATCH)
    first = np.block([[cosine, -sine], [sine, cosine]])
    out = []
    for table in (first, first.T):
        high = table.astype(BF16)
        out.append(high)
        out.append((table - high.astype(np.float64)).astype(BF16))
    return np.stack(out)


def place():
    slab = lax.axis_index("slab")
    strip = lax.axis_index("strip")
    return slab, strip


def greet(slab, strip, slabs, strips, col_tiles, edge):
    group, col = strip // col_tiles, strip % col_tiles
    groups = strips // col_tiles
    barrier = pltpu.get_barrier_semaphore()

    def signal(to_slab, to_strip):
        pl.semaphore_signal(
            barrier, inc=1, device_id={"slab": to_slab, "strip": to_strip}, device_id_type=MESH
        )

    for step in range(1, slabs):
        signal(lax.rem(slab + step, slabs), strip)
    for step in range(1, col_tiles):
        signal(slab, group * col_tiles + lax.rem(col + step, col_tiles))

    def greet_group(other, near, far_first):
        @pl.when(near)
        def _():
            for tile in range(col_tiles):
                signal(slab, other * col_tiles + tile)

        @pl.when(jnp.logical_not(near))
        def _():
            for tile in range(edge):
                signal(slab, other * col_tiles + far_first + tile)

    @pl.when(group > 0)
    def _():
        greet_group(group - 1, col < edge, col_tiles - edge)

    @pl.when(group < groups - 1)
    def _():
        greet_group(group + 1, col >= col_tiles - edge, 0)

    base = slabs - 1 + col_tiles - 1
    above = jnp.where(group > 0, jnp.where(col < edge, col_tiles, edge), 0)
    below = jnp.where(group < groups - 1, jnp.where(col >= col_tiles - edge, col_tiles, edge), 0)
    return barrier, base + above + below


def field_kernel(
    slabs, strips, shear_ref, vol_ref, ext_ref,
    part, slab_in, proj, land, land_edge,
    slab_send, slab_recv, send, recv, edge_send, edge_recv,
):
    depth, rows, width = vol_ref.shape
    wide = width + 2 * RIM
    col_tiles = width // TILE_W
    groups = strips // col_tiles
    edge = RIM // rows
    slab, strip = place()
    group, col = strip // col_tiles, strip % col_tiles
    barrier, peers = greet(slab, strip, slabs, strips, col_tiles, edge)
    lane = lax.broadcasted_iota(jnp.int32, (rows, wide), 1)
    inside = (lane >= RIM) & (lane < RIM + width)
    zeros = jnp.zeros((rows, 2 * RIM), F32)

    def partial(view):
        total = jnp.zeros((rows, wide), F32)
        for z in range(depth):
            layer = jnp.concatenate([vol_ref[z].astype(F32), zeros], 1)
            total = total + pltpu.roll(layer, shear_ref[view, z] + RIM, 1)
        return jnp.where(inside, total, 0.0).astype(BF16)

    copies = []
    for step in range(1, slabs):
        view = lax.rem(slab + step, slabs)
        part[step - 1] = partial(view)
        if step == 1:
            pl.semaphore_wait(barrier, peers)
        copy = pltpu.make_async_remote_copy(
            src_ref=part.at[step - 1], dst_ref=slab_in.at[step - 1],
            send_sem=slab_send.at[step - 1], recv_sem=slab_recv.at[step - 1],
            device_id={"slab": view, "strip": strip}, device_id_type=MESH,
        )
        copy.start()
        copies.append(copy)
    total = partial(slab).astype(F32)
    if slabs == 1:
        pl.semaphore_wait(barrier, peers)
    for step in range(1, slabs):
        copies[step - 1].wait_recv()
        total = total + slab_in[step - 1].astype(F32)
    proj[...] = total.astype(BF16)

    def window(tile):
        return pl.ds(pl.multiple_of(tile * TILE_W, TILE_W), WIN)

    top = (col < edge) & (group > 0)
    bottom = (col >= col_tiles - edge) & (group < groups - 1)
    other = jnp.where(col < edge, group - 1, group + 1)
    slot = jnp.where(col < edge, edge + col, col - (col_tiles - edge))

    def edge_copy(tile):
        return pltpu.make_async_remote_copy(
            src_ref=proj.at[:, pl.ds(tile * TILE_W, WIN)], dst_ref=land_edge.at[slot],
            send_sem=edge_send.at[tile], recv_sem=edge_recv.at[slot],
            device_id={"slab": slab, "strip": other * col_tiles + tile}, device_id_type=MESH,
        )

    @pl.when(top | bottom)
    def _():
        for tile in range(col_tiles):
            edge_copy(tile).start()

    group_copies = []
    for step in range(1, col_tiles):
        tile = lax.rem(col + step, col_tiles)
        copy = pltpu.make_async_remote_copy(
            src_ref=proj.at[:, window(tile)], dst_ref=land.at[step - 1],
            send_sem=send.at[step - 1], recv_sem=recv.at[step - 1],
            device_id={"slab": slab, "strip": group * col_tiles + tile}, device_id_type=MESH,
        )
        copy.start()
        group_copies.append(copy)
    ext_ref[edge + col] = proj[:, window(col)]
    for step in range(1, col_tiles):
        group_copies[step - 1].wait_recv()
        ext_ref[edge + lax.rem(col + col_tiles - step, col_tiles)] = land[step - 1]

    def edge_in(first, place_at, has):
        @pl.when(has)
        def _():
            for k in range(edge):
                pltpu.make_async_remote_copy(
                    src_ref=proj.at[:, pl.ds(0, WIN)], dst_ref=land_edge.at[first + k],
                    send_sem=edge_send.at[0], recv_sem=edge_recv.at[first + k],
                    device_id={"slab": slab, "strip": other * col_tiles}, device_id_type=MESH,
                ).wait_recv()
                ext_ref[place_at + k] = land_edge[first + k]

        @pl.when(jnp.logical_not(has))
        def _():
            for k in range(edge):
                ext_ref[place_at + k] = jnp.zeros((rows, WIN), BF16)

    edge_in(0, 0, group > 0)
    edge_in(edge, edge + col_tiles, group < groups - 1)
    for copy in copies:
        copy.wait_send()
    for copy in group_copies:
        copy.wait_send()

    @pl.when(top | bottom)
    def _():
        for tile in range(col_tiles):
            edge_copy(tile).wait_send()


def cos_sin(x):
    turn = jnp.floor(x * (2.0 / math.pi) + 0.5)
    r = ((x - turn * 1.5703125) - turn * 4.837512969970703125e-4) - turn * 7.54978995489188216e-8
    z = r * r
    s = ((-1.9515295891e-4 * z + 8.3321608736e-3) * z - 1.6666654611e-1) * z * r + r
    c = ((2.443315711809948e-5 * z - 1.388731625493765e-3) * z + 4.166664568298827e-2) * z * z
    c = c - 0.5 * z + 1.0
    quarter = turn.astype(jnp.int32) & 3
    odd = (quarter & 1) == 1
    cos = jnp.where(odd, s, c)
    sin = jnp.where(odd, c, s)
    cos = jnp.where((quarter == 1) | (quarter == 2), -cos, cos)
    sin = jnp.where(quarter >= 2, -sin, sin)
    return cos, sin


def split(x):
    high = x.astype(BF16)
    return high, (x - high.astype(F32)).astype(BF16)


def mm(a, b):
    return jnp.dot(a, b, preferred_element_type=F32)


def patch_kernel(pos_ref, ext_ref, probe_ref, meas_ref, tab_ref, out_ref, cosf, sinf, acc):
    slots, rows, _ = ext_ref.shape
    count = meas_ref.shape[0]
    halves = WIN // PATCH

    def right(x, which):
        high, low = split(x)
        t_high, t_low = tab_ref[2 * which], tab_ref[2 * which + 1]
        return mm(high, t_high) + (mm(low, t_high) + mm(high, t_low))

    def left(which, x):
        high, low = split(x)
        t_high, t_low = tab_ref[2 * which], tab_ref[2 * which + 1]
        return mm(t_high, high) + (mm(t_high, low) + mm(t_low, high))

    def trig(j, _):
        cos, sin = cos_sin(ext_ref[j].astype(F32))
        at = pl.ds(pl.multiple_of(j * rows, rows), rows)
        for h in range(halves):
            cosf[h, at, :] = cos[:, h * PATCH : (h + 1) * PATCH]
            sinf[h, at, :] = sin[:, h * PATCH : (h + 1) * PATCH]
            acc[h, at, :] = jnp.zeros((rows, PATCH), F32)
        return 0

    lax.fori_loop(0, slots, trig, 0)

    def cut(field, row, by):
        strips = [field[h, pl.ds(row, PATCH), :] for h in range(halves)]
        return pltpu.roll(jnp.concatenate(strips, 1), by, 1)[:, :PATCH]

    def pair(i, _):
        probe_re, probe_im = probe_ref[0], probe_ref[1]
        where, waves, cuts = [], [], []
        for k in range(2):
            row = pos_ref[2 * i + k, 0] + RIM
            lane = pos_ref[2 * i + k, 1] + RIM
            back_by = (WIN - lane) & (WIN - 1)
            cos = cut(cosf, row, back_by)
            sin = cut(sinf, row, back_by)
            where.append((row, lane))
            cuts.append((cos, sin))
            waves.append(
                jnp.concatenate(
                    [probe_re * cos - probe_im * sin, probe_re * sin + probe_im * cos], 1
                )
            )
        half = right(jnp.concatenate(waves, 0), 0)
        half = jnp.concatenate(
            [
                jnp.concatenate([half[:PATCH, :PATCH], half[PATCH:, :PATCH]], 1),
                jnp.concatenate([half[:PATCH, PATCH:], half[PATCH:, PATCH:]], 1),
            ],
            0,
        )
        far = left(1, half)
        far_re, far_im = far[:PATCH], far[PATCH:]
        meas = jnp.concatenate([meas_ref[2 * i], meas_ref[2 * i + 1]], 1).astype(F32)
        weight = GRAD_SCALE * (far_re * far_re + far_im * far_im - meas)
        half = left(0, jnp.concatenate([weight * far_re, weight * far_im], 0))
        half = jnp.concatenate(
            [
                jnp.concatenate([half[:PATCH, :PATCH], half[PATCH:, :PATCH]], 1),
                jnp.concatenate([half[:PATCH, PATCH:], half[PATCH:, PATCH:]], 1),
            ],
            0,
        )
        back = right(half, 1)
        for k in range(2):
            row, lane = where[k]
            cos, sin = cuts[k]
            back_re = back[k * PATCH : (k + 1) * PATCH, :PATCH]
            back_im = back[k * PATCH : (k + 1) * PATCH, PATCH:]
            grad_re = probe_re * back_re + probe_im * back_im
            grad_im = probe_re * back_im - probe_im * back_re
            grad = cos * grad_im - sin * grad_re
            grad = jnp.concatenate([grad, jnp.zeros_like(grad)], 1)
            at = pl.ds(row, PATCH)
            grad = pltpu.roll(grad, lane, 1)
            for h in range(halves):
                acc[h, at, :] = acc[h, at, :] + grad[:, h * PATCH : (h + 1) * PATCH]
        return 0

    lax.fori_loop(0, count // 2, pair, 0)

    def finish(j, _):
        at = pl.ds(pl.multiple_of(j * rows, rows), rows)
        out_ref[j] = jnp.concatenate([acc[h, at, :] for h in range(halves)], 1).astype(BF16)
        return 0

    lax.fori_loop(0, slots, finish, 0)


def back_kernel(
    slabs, strips, shear_ref, grad_ref, out_ref,
    land, land_edge, total, own, slab_in,
    slab_send, slab_recv, send, recv, edge_send, edge_recv,
):
    depth, rows, width = out_ref.shape
    wide = width + 2 * RIM
    col_tiles = width // TILE_W
    groups = strips // col_tiles
    edge = RIM // rows
    slab, strip = place()
    group, col = strip // col_tiles, strip % col_tiles
    barrier, peers = greet(slab, strip, slabs, strips, col_tiles, edge)
    pl.semaphore_wait(barrier, peers)

    def edge_copy(k, other, source, owner):
        return pltpu.make_async_remote_copy(
            src_ref=grad_ref.at[source], dst_ref=land_edge.at[col],
            send_sem=edge_send.at[k], recv_sem=edge_recv.at[col],
            device_id={"slab": slab, "strip": other * col_tiles + owner}, device_id_type=MESH,
        )

    def edge_copies(act):
        @pl.when(group > 0)
        def _():
            for k in range(edge):
                act(edge_copy(k, group - 1, k, col_tiles - edge + k))

        @pl.when(group < groups - 1)
        def _():
            for k in range(edge):
                act(edge_copy(edge + k, group + 1, edge + col_tiles + k, k))

    edge_copies(lambda copy: copy.start())
    group_copies = []
    for step in range(1, col_tiles):
        tile = lax.rem(col + step, col_tiles)
        copy = pltpu.make_async_remote_copy(
            src_ref=grad_ref.at[edge + tile], dst_ref=land.at[step - 1],
            send_sem=send.at[step - 1], recv_sem=recv.at[step - 1],
            device_id={"slab": slab, "strip": group * col_tiles + tile}, device_id_type=MESH,
        )
        copy.start()
        group_copies.append(copy)
    total[...] = jnp.zeros((rows, wide), F32)

    def window(tile):
        return pl.ds(pl.multiple_of(tile * TILE_W, TILE_W), WIN)

    total[:, window(col)] = total[:, window(col)] + grad_ref[edge + col].astype(F32)
    for step in range(1, col_tiles):
        group_copies[step - 1].wait_recv()
        at = window(lax.rem(col + col_tiles - step, col_tiles))
        total[:, at] = total[:, at] + land[step - 1].astype(F32)

    has_edge = ((col < edge) & (group > 0)) | ((col >= col_tiles - edge) & (group < groups - 1))
    other = jnp.where(col < edge, group - 1, group + 1)

    @pl.when(has_edge)
    def _():
        for tile in range(col_tiles):
            pltpu.make_async_remote_copy(
                src_ref=grad_ref.at[0], dst_ref=land_edge.at[tile],
                send_sem=edge_send.at[0], recv_sem=edge_recv.at[tile],
                device_id={"slab": slab, "strip": other * col_tiles + tile}, device_id_type=MESH,
            ).wait_recv()
            at = window(tile)
            total[:, at] = total[:, at] + land_edge[tile].astype(F32)

    lane = lax.broadcasted_iota(jnp.int32, (rows, wide), 1)
    inside = (lane >= RIM) & (lane < RIM + width)
    mine = jnp.where(inside, total[...], 0.0).astype(BF16)
    own[...] = mine
    copies = []
    for step in range(1, slabs):
        copy = pltpu.make_async_remote_copy(
            src_ref=own, dst_ref=slab_in.at[step - 1],
            send_sem=slab_send.at[step - 1], recv_sem=slab_recv.at[step - 1],
            device_id={"slab": lax.rem(slab + step, slabs), "strip": strip}, device_id_type=MESH,
        )
        copy.start()
        copies.append(copy)

    def sheared(field, view, z):
        by = lax.rem(wide - RIM - shear_ref[view, z], wide)
        return pltpu.roll(field, by, 1)[:, :width]

    results = [sheared(mine.astype(F32), slab, z) for z in range(depth)]
    for step in range(1, slabs):
        copies[step - 1].wait_recv()
        field = slab_in[step - 1].astype(F32)
        view = lax.rem(slab + slabs - step, slabs)
        results = [results[z] + sheared(field, view, z) for z in range(depth)]
    for z in range(depth):
        out_ref[z] = results[z].astype(BF16)
    for copy in copies:
        copy.wait_send()
    for copy in group_copies:
        copy.wait_send()
    edge_copies(lambda copy: copy.wait_send())


def local(slabs, strips, volume, shear, probe, positions, measured):
    depth, rows, width = volume.shape
    col_tiles = width // TILE_W
    wide = width + 2 * RIM
    edge = RIM // rows
    slots = col_tiles + 2 * edge
    others = max(slabs - 1, 1)
    vmem = pl.BlockSpec(memory_space=pltpu.VMEM)
    smem = pl.BlockSpec(memory_space=pltpu.SMEM)
    dma = pltpu.SemaphoreType.DMA
    ext = pl.pallas_call(
        functools.partial(field_kernel, slabs, strips),
        out_shape=jax.ShapeDtypeStruct((slots, rows, WIN), BF16),
        in_specs=[smem, vmem],
        out_specs=vmem,
        scratch_shapes=[
            pltpu.VMEM((others, rows, wide), BF16),
            pltpu.VMEM((others, rows, wide), BF16),
            pltpu.VMEM((rows, wide), BF16),
            pltpu.VMEM((col_tiles - 1, rows, WIN), BF16),
            pltpu.VMEM((2 * edge, rows, WIN), BF16),
            dma((others,)), dma((others,)),
            dma((col_tiles - 1,)), dma((col_tiles - 1,)),
            dma((col_tiles,)), dma((2 * edge,)),
        ],
        compiler_params=pltpu.CompilerParams(collective_id=0, has_side_effects=True),
        name="field",
    )(shear, volume)
    tables = jnp.asarray(dft_tables())
    grads = pl.pallas_call(
        patch_kernel,
        out_shape=jax.ShapeDtypeStruct((slots, rows, WIN), BF16),
        in_specs=[smem, vmem, vmem, vmem, vmem],
        out_specs=vmem,
        scratch_shapes=[pltpu.VMEM((WIN // PATCH, slots * rows, PATCH), F32) for _ in range(3)],
        name="patches",
    )(positions[0, 0], ext, probe, measured[0, 0], tables)
    return pl.pallas_call(
        functools.partial(back_kernel, slabs, strips),
        out_shape=jax.ShapeDtypeStruct(volume.shape, BF16),
        in_specs=[smem, vmem],
        out_specs=vmem,
        scratch_shapes=[
            pltpu.VMEM((col_tiles - 1, rows, WIN), BF16),
            pltpu.VMEM((col_tiles, rows, WIN), BF16),
            pltpu.VMEM((rows, wide), F32),
            pltpu.VMEM((rows, wide), BF16),
            pltpu.VMEM((others, rows, wide), BF16),
            dma((others,)), dma((others,)),
            dma((col_tiles - 1,)), dma((col_tiles - 1,)),
            dma((2 * edge,)), dma((col_tiles,)),
        ],
        compiler_params=pltpu.CompilerParams(collective_id=1, has_side_effects=True),
        name="back",
    )(shear, grads)


def solution(mesh):
    placed = (
        P("slab", "strip", None),
        P(None, "slab"),
        P(),
        P("slab", "strip", None, None),
        P("slab", "strip", None, None, None),
    )
    return jax.shard_map(
        functools.partial(local, mesh.shape["slab"], mesh.shape["strip"]),
        mesh=mesh, in_specs=placed, out_specs=P("slab", "strip", None), check_vma=False,
    )
```

profile of v0, /device:TPU:0, one launch (start us, length us, event | category | flops | bytes accessed | tf_op | source)
XLA Modules:
  0.0 44.4 jit_solution(483924750750908859)
XLA Ops:
  0.0 0.0 copy-start
  0.0 0.7 %copy-done = s32[1,1,16,2]{2,3,1,0:T(2,128)S(1)} copy-done((s32[1,1,16,2]{2,3,1,0:T(2,128)S(1)}, s32[1,1,16,2]{2,3,1,0:T(2,128)}, u32[]{:S(2)}) %copy-start) | copy-done | bytes 152
  0.7 0.7 %copy.7.pos_ref = s32[16,2]{1,0:T(8,128)} copy(s32[16,2]{0,1:T(2,128)S(1)} %bitcast.3) | data formatting | bytes 256 | tf_op jit(solution)/shard_map/squeeze | solution.py:446
  1.4 14.5 %field.1.ext_ref = bf16[12,32,256]{2,1,0:T(8,128)(2,1)} custom-call(s32[2,4]{1,0:T(2,128)} %shear_ref.3, bf16[4,32,1024]{2,1,0:T(8,128)(2,1)} %vol_ref.1), custom_call_target="tpu_custom_call" | custom-call | tf_op jit(solution)/shard_map/field/pallas_call | solution.py:420
  15.8 15.0 %patches.1.grad_ref = bf16[12,32,256]{2,1,0:T(8,128)(2,1)} custom-call(s32[16,2]{1,0:T(8,128)} %copy.7.pos_ref, bf16[12,32,256]{2,1,0:T(8,128)(2,1)} %field.1.ext_ref, f32[2,128,128]{2,1,0:T(8,128)} %probe_ref.1, bf16[16,128,128]{2,1,0:T(8,128)(2,1)} %bitcast.2, bf16[4,256,256]{2,1,0:T(8,128)(2,1)} %constant.2.clone.tab_ref), custom_call_target="tpu_custom_call" | custom-call | tf_op jit(solution)/shard_map/patches/pallas_call | solution.py:439
  30.8 11.9 %back.1 = bf16[4,32,1024]{2,1,0:T(8,128)(2,1)} custom-call(s32[2,4]{1,0:T(2,128)} %shear_ref.3, bf16[12,32,256]{2,1,0:T(8,128)(2,1)} %patches.1.grad_ref), custom_call_target="tpu_custom_call" | custom-call | tf_op jit(solution)/shard_map/back/pallas_call | solution.py:447
  42.7 1.7 %copy.9 = bf16[4,32,1024]{2,1,0:T(8,128)(2,1)} copy(bf16[4,32,1024]{2,1,0:T(8,128)(2,1)} %back.1) | data formatting | bytes 524288
Async XLA Ops:
  0.0 0.7 %copy-start = (s32[1,1,16,2]{2,3,1,0:T(2,128)S(1)}, s32[1,1,16,2]{2,3,1,0:T(2,128)}, u32[]{:S(2)}) copy-start(s32[1,1,16,2]{2,3,1,0:T(2,128)} %param.9) | copy-start | bytes 388
where the time goes:
time: 44.6 us; the launch traced here: 44.4 us
  Pallas kernels  41.4 us (93%)
  local copies, waits for them, and re-layouts  3.02 us (7%)
    pallas_call x1, Pallas kernels, local(): pl.pallas_call(patch_kernel, out_shape=jax.ShapeDtypeStruct((slots, rows,...  15 us
    pallas_call x1, Pallas kernels, local(): pl.pallas_call(functools.partial(field_kernel, slabs, strips), out_shape=...  14.5 us
    pallas_call x1, Pallas kernels, local(): pl.pallas_call(functools.partial(back_kernel, slabs, strips), out_shape=j...  11.9 us
    unnamed x3, local copies, waits for them, and re-layouts  2.35 us

commit v1 on v0

--- a/solution.py
+++ b/solution.py
@@ -14,6 +14,7 @@
 RIM = PATCH // 2
 WIN = TILE_W + 2 * RIM
 GRAD_SCALE = 0.125
+PAIRS = 4
 MESH = pl.DeviceIdType.MESH
 F32 = jnp.float32
 BF16 = jnp.bfloat16
@@ -219,14 +220,29 @@
     halves = WIN // PATCH
 
     def right(x, which):
+        return mm(x.astype(BF16), tab_ref[2 * which])
+
+    def left(which, x):
+        return mm(tab_ref[2 * which], x.astype(BF16))
+
+    def right3(x, which):
         high, low = split(x)
         t_high, t_low = tab_ref[2 * which], tab_ref[2 * which + 1]
         return mm(high, t_high) + (mm(low, t_high) + mm(high, t_low))
 
-    def left(which, x):
+    def left3(which, x):
         high, low = split(x)
         t_high, t_low = tab_ref[2 * which], tab_ref[2 * which + 1]
         return mm(t_high, high) + (mm(t_high, low) + mm(t_low, high))
+
+    def regroup(x):
+        return jnp.concatenate(
+            [
+                jnp.concatenate([x[:PATCH, :PATCH], x[PATCH:, :PATCH]], 1),
+                jnp.concatenate([x[:PATCH, PATCH:], x[PATCH:, PATCH:]], 1),
+            ],
+            0,
+        )
 
     def trig(j, _):
         cos, sin = cos_sin(ext_ref[j].astype(F32))
@@ -237,54 +253,46 @@
             acc[h, at, :] = jnp.zeros((rows, PATCH), F32)
         return 0
 
-    lax.fori_loop(0, slots, trig, 0)
+    lax.fori_loop(0, slots, trig, 0, unroll=2)
 
     def cut(field, row, by):
         strips = [field[h, pl.ds(row, PATCH), :] for h in range(halves)]
         return pltpu.roll(jnp.concatenate(strips, 1), by, 1)[:, :PATCH]
 
-    def pair(i, _):
+    def pairs(j, _):
         probe_re, probe_im = probe_ref[0], probe_ref[1]
-        where, waves, cuts = [], [], []
-        for k in range(2):
-            row = pos_ref[2 * i + k, 0] + RIM
-            lane = pos_ref[2 * i + k, 1] + RIM
-            back_by = (WIN - lane) & (WIN - 1)
-            cos = cut(cosf, row, back_by)
-            sin = cut(sinf, row, back_by)
-            where.append((row, lane))
-            cuts.append((cos, sin))
-            waves.append(
-                jnp.concatenate(
-                    [probe_re * cos - probe_im * sin, probe_re * sin + probe_im * cos], 1
-                )
-            )
-        half = right(jnp.concatenate(waves, 0), 0)
-        half = jnp.concatenate(
-            [
-                jnp.concatenate([half[:PATCH, :PATCH], half[PATCH:, :PATCH]], 1),
-                jnp.concatenate([half[:PATCH, PATCH:], half[PATCH:, PATCH:]], 1),
-            ],
-            0,
-        )
-        far = left(1, half)
-        far_re, far_im = far[:PATCH], far[PATCH:]
-        meas = jnp.concatenate([meas_ref[2 * i], meas_ref[2 * i + 1]], 1).astype(F32)
-        weight = GRAD_SCALE * (far_re * far_re + far_im * far_im - meas)
-        half = left(0, jnp.concatenate([weight * far_re, weight * far_im], 0))
-        half = jnp.concatenate(
-            [
-                jnp.concatenate([half[:PATCH, :PATCH], half[PATCH:, :PATCH]], 1),
-                jnp.concatenate([half[:PATCH, PATCH:], half[PATCH:, PATCH:]], 1),
-            ],
-            0,
-        )
-        back = right(half, 1)
-        for k in range(2):
-            row, lane = where[k]
-            cos, sin = cuts[k]
-            back_re = back[k * PATCH : (k + 1) * PATCH, :PATCH]
-            back_im = back[k * PATCH : (k + 1) * PATCH, PATCH:]
+        members = [PAIRS * j + u for u in range(PAIRS)]
+        where, cuts, halves_in = [], [], []
+        for i in members:
+            waves = []
+            for k in range(2):
+                row = pos_ref[0, 2 * i + k] + RIM
+                lane = pos_ref[1, 2 * i + k] + RIM
+                back_by = (WIN - lane) & (WIN - 1)
+                cos = cut(cosf, row, back_by)
+                sin = cut(sinf, row, back_by)
+                where.append((row, lane))
+                cuts.append((cos, sin))
+                wave_re = probe_re * cos - probe_im * sin
+                wave_im = probe_re * sin + probe_im * cos
+                waves.append(jnp.concatenate([wave_re, wave_im], 1))
+            halves_in.append(jnp.concatenate(waves, 0))
+        half = [regroup(right3(x, 0)) for x in halves_in]
+        far = [left3(1, x) for x in half]
+        weighted = []
+        for i, x in zip(members, far):
+            far_re, far_im = x[:PATCH], x[PATCH:]
+            meas = jnp.concatenate([meas_ref[2 * i], meas_ref[2 * i + 1]], 1).astype(F32)
+            weight = GRAD_SCALE * (far_re * far_re + far_im * far_im - meas)
+            weighted.append(jnp.concatenate([weight * far_re, weight * far_im], 0))
+        half = [regroup(left(0, x)) for x in weighted]
+        back = [right(x, 1) for x in half]
+        for u in range(2 * PAIRS):
+            row, lane = where[u]
+            cos, sin = cuts[u]
+            k = u % 2
+            back_re = back[u // 2][k * PATCH : (k + 1) * PATCH, :PATCH]
+            back_im = back[u // 2][k * PATCH : (k + 1) * PATCH, PATCH:]
             grad_re = probe_re * back_re + probe_im * back_im
             grad_im = probe_re * back_im - probe_im * back_re
             grad = cos * grad_im - sin * grad_re
@@ -295,7 +303,7 @@
                 acc[h, at, :] = acc[h, at, :] + grad[:, h * PATCH : (h + 1) * PATCH]
         return 0
 
-    lax.fori_loop(0, count // 2, pair, 0)
+    lax.fori_loop(0, count // (2 * PAIRS), pairs, 0)
 
     def finish(j, _):
         at = pl.ds(pl.multiple_of(j * rows, rows), rows)
@@ -306,12 +314,12 @@
 
 
 def back_kernel(
-    slabs, strips, shear_ref, grad_ref, out_ref,
+    slabs, strips, grad_ref, out_ref,
     land, land_edge, total, own, slab_in,
     slab_send, slab_recv, send, recv, edge_send, edge_recv,
 ):
-    depth, rows, width = out_ref.shape
-    wide = width + 2 * RIM
+    _, rows, wide = out_ref.shape
+    width = wide - 2 * RIM
     col_tiles = width // TILE_W
     groups = strips // col_tiles
     edge = RIM // rows
@@ -388,23 +396,26 @@
         copy.start()
         copies.append(copy)
 
-    def sheared(field, view, z):
-        by = lax.rem(wide - RIM - shear_ref[view, z], wide)
-        return pltpu.roll(field, by, 1)[:, :width]
-
-    results = [sheared(mine.astype(F32), slab, z) for z in range(depth)]
+    out_ref[slab] = mine
     for step in range(1, slabs):
         copies[step - 1].wait_recv()
-        field = slab_in[step - 1].astype(F32)
-        view = lax.rem(slab + slabs - step, slabs)
-        results = [results[z] + sheared(field, view, z) for z in range(depth)]
-    for z in range(depth):
-        out_ref[z] = results[z].astype(BF16)
+        out_ref[lax.rem(slab + slabs - step, slabs)] = slab_in[step - 1]
     for copy in copies:
         copy.wait_send()
     for copy in group_copies:
         copy.wait_send()
     edge_copies(lambda copy: copy.wait_send())
+
+
+def spread_kernel(shear_ref, fields_ref, out_ref):
+    depth, rows, width = out_ref.shape
+    views, _, wide = fields_ref.shape
+    for z in range(depth):
+        result = jnp.zeros((rows, width), F32)
+        for view in range(views):
+            by = lax.rem(wide - RIM - shear_ref[view, z], wide)
+            result = result + pltpu.roll(fields_ref[view].astype(F32), by, 1)[:, :width]
+        out_ref[z] = result.astype(BF16)
 
 
 def local(slabs, strips, volume, shear, probe, positions, measured):
@@ -443,11 +454,11 @@
         out_specs=vmem,
         scratch_shapes=[pltpu.VMEM((WIN // PATCH, slots * rows, PATCH), F32) for _ in range(3)],
         name="patches",
-    )(positions[0, 0], ext, probe, measured[0, 0], tables)
-    return pl.pallas_call(
+    )(positions[0, 0].T, ext, probe, measured[0, 0], tables)
+    fields = pl.pallas_call(
         functools.partial(back_kernel, slabs, strips),
-        out_shape=jax.ShapeDtypeStruct(volume.shape, BF16),
-        in_specs=[smem, vmem],
+        out_shape=jax.ShapeDtypeStruct((slabs, rows, wide), BF16),
+        in_specs=[vmem],
         out_specs=vmem,
         scratch_shapes=[
             pltpu.VMEM((col_tiles - 1, rows, WIN), BF16),
@@ -461,7 +472,14 @@
         ],
         compiler_params=pltpu.CompilerParams(collective_id=1, has_side_effects=True),
         name="back",
-    )(shear, grads)
+    )(grads)
+    return pl.pallas_call(
+        spread_kernel,
+        out_shape=jax.ShapeDtypeStruct(volume.shape, BF16),
+        in_specs=[smem, vmem],
+        out_specs=vmem,
+        name="spread",
+    )(shear, fields)
 
 
 def solution(mesh):

time: 44.6 us -> 34.7 us (0.78)
  Pallas kernels: 41.4 us -> 34.5 us
  local copies, waits for them, and re-layouts: 3.02 us -> 0 us
    pallas_call x1, Pallas kernels: 15 us -> 6.54 us  [local(): pl.pallas_call(patch_kernel, out_shape=jax.ShapeDtypeStruct((slots, rows,...]
    unnamed x3 -> x0, local copies, waits for them, and re-layouts: 2.35 us -> none
    pallas_call x0 -> x1, Pallas kernels: none -> 2 us  [local(): pl.pallas_call(spread_kernel, out_shape=jax.ShapeDtypeStruct(volume.shape...]
    squeeze x1 -> x0, local copies, waits for them, and re-layouts: 0.68 us -> none  [local(): positions[0, 0]]
where the time goes in v1:
time: 34.7 us; the launch traced here: 34.5 us
  Pallas kernels  34.5 us (99%)
    pallas_call x1, Pallas kernels, local(): pl.pallas_call(functools.partial(field_kernel, slabs, strips), out_shape=...  14.5 us
    pallas_call x1, Pallas kernels, local(): pl.pallas_call(functools.partial(back_kernel, slabs, strips), out_shape=j...  11.5 us
    pallas_call x1, Pallas kernels, local(): pl.pallas_call(patch_kernel, out_shape=jax.ShapeDtypeStruct((slots, rows,...  6.54 us
    pallas_call x1, Pallas kernels, local(): pl.pallas_call(spread_kernel, out_shape=jax.ShapeDtypeStruct(volume.shape...  2 us

profile of v1, /device:TPU:0, one launch (start us, length us, event | category | flops | bytes accessed | tf_op | source)
XLA Modules:
  0.0 34.5 jit_solution(11942819443413180663)
XLA Ops:
  0.0 14.5 %field.1.ext_ref = bf16[12,32,256]{2,1,0:T(8,128)(2,1)} custom-call(s32[2,4]{1,0:T(2,128)} %shear_ref.3, bf16[4,32,1024]{2,1,0:T(8,128)(2,1)} %vol_ref.1), custom_call_target="tpu_custom_call" | custom-call | tf_op jit(solution)/shard_map/field/pallas_call | solution.py:431
  14.5 6.5 %patches.1.grad_ref = bf16[12,32,256]{2,1,0:T(8,128)(2,1)} custom-call(s32[2,16]{1,0:T(2,128)} %bitcast.5, bf16[12,32,256]{2,1,0:T(8,128)(2,1)} %field.1.ext_ref, f32[2,128,128]{2,1,0:T(8,128)} %probe_ref.1, bf16[16,128,128]{2,1,0:T(8,128)(2,1)} %bitcast.4, bf16[4,256,256]{2,1,0:T(8,128)(2,1)} %constant.2.clone.tab_ref), custom_call_target="tpu_custom_call" | custom-call | tf_op jit(solution)/shard_map/patches/pallas_call | solution.py:450
  21.0 11.5 %back.1.fields_ref = bf16[2,32,1152]{2,1,0:T(8,128)(2,1)} custom-call(bf16[12,32,256]{2,1,0:T(8,128)(2,1)} %patches.1.grad_ref), custom_call_target="tpu_custom_call" | custom-call | tf_op jit(solution)/shard_map/back/pallas_call | solution.py:458
  32.5 2.0 %spread.1 = bf16[4,32,1024]{2,1,0:T(8,128)(2,1)} custom-call(s32[2,4]{1,0:T(2,128)} %shear_ref.3, bf16[2,32,1152]{2,1,0:T(8,128)(2,1)} %back.1.fields_ref), custom_call_target="tpu_custom_call" | custom-call | tf_op jit(solution)/shard_map/spread/pallas_call | solution.py:476

commit v2 on v1

v2 whole, which is shorter than its diff:
```python
import functools
import math

import jax
import jax.numpy as jnp
import numpy as np
from jax import lax
from jax.experimental import pallas as pl
from jax.experimental.pallas import tpu as pltpu
from jax.sharding import PartitionSpec as P

TILE_W = 128
PATCH = 128
RIM = PATCH // 2
WIN = TILE_W + 2 * RIM
GRAD_SCALE = 0.125
PAIRS = 4
MESH = pl.DeviceIdType.MESH
F32 = jnp.float32
BF16 = jnp.bfloat16


def dft_tables():
    index = np.arange(PATCH)
    angle = 2.0 * math.pi * ((index[:, None] * index[None, :]) % PATCH) / PATCH
    cosine = np.cos(angle) / math.sqrt(PATCH)
    sine = np.sin(angle) / math.sqrt(PATCH)
    first = np.block([[cosine, -sine], [sine, cosine]])
    out = []
    for table in (first, first.T):
        high = table.astype(BF16)
        out.append(high)
        out.append((table - high.astype(np.float64)).astype(BF16))
    return np.stack(out)


def place():
    slab = lax.axis_index("slab")
    strip = lax.axis_index("strip")
    return slab, strip


def greet(slab, strip, slabs, strips, col_tiles, edge):
    group, col = strip // col_tiles, strip % col_tiles
    groups = strips // col_tiles
    barrier = pltpu.get_barrier_semaphore()

    def signal(to_slab, to_strip):
        pl.semaphore_signal(
            barrier, inc=1, device_id={"slab": to_slab, "strip": to_strip}, device_id_type=MESH
        )

    for step in range(1, slabs):
        signal(lax.rem(slab + step, slabs), strip)
    for step in range(1, col_tiles):
        signal(slab, group * col_tiles + lax.rem(col + step, col_tiles))

    def greet_group(other, near, far_first):
        @pl.when(near)
        def _():
            for tile in range(col_tiles):
                signal(slab, other * col_tiles + tile)

        @pl.when(jnp.logical_not(near))
        def _():
            for tile in range(edge):
                signal(slab, other * col_tiles + far_first + tile)

    @pl.when(group > 0)
    def _():
        greet_group(group - 1, col < edge, col_tiles - edge)

    @pl.when(group < groups - 1)
    def _():
        greet_group(group + 1, col >= col_tiles - edge, 0)

    base = slabs - 1 + col_tiles - 1
    above = jnp.where(group > 0, jnp.where(col < edge, col_tiles, edge), 0)
    below = jnp.where(group < groups - 1, jnp.where(col >= col_tiles - edge, col_tiles, edge), 0)
    return barrier, base + above + below


def cos_sin(x):
    turn = jnp.floor(x * (2.0 / math.pi) + 0.5)
    r = ((x - turn * 1.5703125) - turn * 4.837512969970703125e-4) - turn * 7.54978995489188216e-8
    z = r * r
    s = ((-1.9515295891e-4 * z + 8.3321608736e-3) * z - 1.6666654611e-1) * z * r + r
    c = ((2.443315711809948e-5 * z - 1.388731625493765e-3) * z + 4.166664568298827e-2) * z * z
    c = c - 0.5 * z + 1.0
    quarter = turn.astype(jnp.int32) & 3
    odd = (quarter & 1) == 1
    cos = jnp.where(odd, s, c)
    sin = jnp.where(odd, c, s)
    cos = jnp.where((quarter == 1) | (quarter == 2), -cos, cos)
    sin = jnp.where(quarter >= 2, -sin, sin)
    return cos, sin


def split(x):
    high = x.astype(BF16)
    return high, (x - high.astype(F32)).astype(BF16)


def mm(a, b):
    return jnp.dot(a, b, preferred_element_type=F32)


def grad_kernel(
    slabs, strips, shear_ref, pos_ref, vol_ref, probe_any, meas_any, tab_any, out_ref,
    probe_ref, meas_ref, tab_ref, load_sem,
    part, slab_in, proj, land, land_edge,
    cosf, sinf, acc, grad_ref, grad_land, grad_edge, total, own, grad_slab,
    slab_send, slab_recv, send, recv, edge_send, edge_recv,
    b_slab_send, b_slab_recv, b_send, b_recv, b_edge_send, b_edge_recv,
):
    pairs_of = ((probe_any, probe_ref), (meas_any, meas_ref), (tab_any, tab_ref))
    loads = [pltpu.make_async_copy(a, b, load_sem.at[k]) for k, (a, b) in enumerate(pairs_of)]
    for load in loads:
        load.start()
    depth, rows, width = vol_ref.shape
    wide = width + 2 * RIM
    col_tiles = width // TILE_W
    groups = strips // col_tiles
    edge = RIM // rows
    slots = col_tiles + 2 * edge
    halves = WIN // PATCH
    slab, strip = place()
    group, col = strip // col_tiles, strip % col_tiles
    barrier, peers = greet(slab, strip, slabs, strips, col_tiles, edge)
    lane = lax.broadcasted_iota(jnp.int32, (rows, wide), 1)
    inside = (lane >= RIM) & (lane < RIM + width)
    zeros = jnp.zeros((rows, 2 * RIM), F32)

    def put(field, at, value):
        for h in range(halves):
            field[h, at, :] = value[:, h * PATCH : (h + 1) * PATCH]

    def trig(place_at, phase):
        cos, sin = cos_sin(phase.astype(F32))
        at = pl.ds(pl.multiple_of(place_at * rows, rows), rows)
        put(cosf, at, cos)
        put(sinf, at, sin)

    def partial(view):
        total = jnp.zeros((rows, wide), F32)
        for z in range(depth):
            layer = jnp.concatenate([vol_ref[z].astype(F32), zeros], 1)
            total = total + pltpu.roll(layer, shear_ref[view, z] + RIM, 1)
        return jnp.where(inside, total, 0.0).astype(BF16)

    copies = []
    for step in range(1, slabs):
        view = lax.rem(slab + step, slabs)
        part[step - 1] = partial(view)
        if step == 1:
            pl.semaphore_wait(barrier, peers)
        copy = pltpu.make_async_remote_copy(
            src_ref=part.at[step - 1], dst_ref=slab_in.at[step - 1],
            send_sem=slab_send.at[step - 1], recv_sem=slab_recv.at[step - 1],
            device_id={"slab": view, "strip": strip}, device_id_type=MESH,
        )
        copy.start()
        copies.append(copy)
    summed = partial(slab).astype(F32)
    if slabs == 1:
        pl.semaphore_wait(barrier, peers)
    for step in range(1, slabs):
        copies[step - 1].wait_recv()
        summed = summed + slab_in[step - 1].astype(F32)
    proj[...] = summed.astype(BF16)

    def window(tile):
        return pl.ds(pl.multiple_of(tile * TILE_W, TILE_W), WIN)

    top = (col < edge) & (group > 0)
    bottom = (col >= col_tiles - edge) & (group < groups - 1)
    other = jnp.where(col < edge, group - 1, group + 1)
    slot = jnp.where(col < edge, edge + col, col - (col_tiles - edge))

    def edge_copy(tile):
        return pltpu.make_async_remote_copy(
            src_ref=proj.at[:, pl.ds(tile * TILE_W, WIN)], dst_ref=land_edge.at[slot],
            send_sem=edge_send.at[tile], recv_sem=edge_recv.at[slot],
            device_id={"slab": slab, "strip": other * col_tiles + tile}, device_id_type=MESH,
        )

    @pl.when(top | bottom)
    def _():
        for tile in range(col_tiles):
            edge_copy(tile).start()

    group_copies = []
    for step in range(1, col_tiles):
        tile = lax.rem(col + step, col_tiles)
        copy = pltpu.make_async_remote_copy(
            src_ref=proj.at[:, window(tile)], dst_ref=land.at[step - 1],
            send_sem=send.at[step - 1], recv_sem=recv.at[step - 1],
            device_id={"slab": slab, "strip": group * col_tiles + tile}, device_id_type=MESH,
        )
        copy.start()
        group_copies.append(copy)
    trig(edge + col, proj[:, window(col)])
    acc[...] = jnp.zeros_like(acc)
    for step in range(1, col_tiles):
        group_copies[step - 1].wait_recv()
        trig(edge + lax.rem(col + col_tiles - step, col_tiles), land[step - 1])

    def edge_in(first, place_at, has):
        @pl.when(has)
        def _():
            for k in range(edge):
                pltpu.make_async_remote_copy(
                    src_ref=proj.at[:, pl.ds(0, WIN)], dst_ref=land_edge.at[first + k],
                    send_sem=edge_send.at[0], recv_sem=edge_recv.at[first + k],
                    device_id={"slab": slab, "strip": other * col_tiles}, device_id_type=MESH,
                ).wait_recv()
                trig(place_at + k, land_edge[first + k])

        @pl.when(jnp.logical_not(has))
        def _():
            for k in range(edge):
                at = pl.ds((place_at + k) * rows, rows)
                put(cosf, at, jnp.ones((rows, WIN), F32))
                put(sinf, at, jnp.zeros((rows, WIN), F32))

    edge_in(0, 0, group > 0)
    edge_in(edge, edge + col_tiles, group < groups - 1)

    for load in loads:
        load.wait()
    count = meas_ref.shape[0]

    def right(x, which):
        return mm(x.astype(BF16), tab_ref[2 * which])

    def left(which, x):
        return mm(tab_ref[2 * which], x.astype(BF16))

    def right3(x, which):
        high, low = split(x)
        t_high, t_low = tab_ref[2 * which], tab_ref[2 * which + 1]
        return mm(high, t_high) + (mm(low, t_high) + mm(high, t_low))

    def left3(which, x):
        high, low = split(x)
        t_high, t_low = tab_ref[2 * which], tab_ref[2 * which + 1]
        return mm(t_high, high) + (mm(t_high, low) + mm(t_low, high))

    def regroup(x):
        return jnp.concatenate(
            [
                jnp.concatenate([x[:PATCH, :PATCH], x[PATCH:, :PATCH]], 1),
                jnp.concatenate([x[:PATCH, PATCH:], x[PATCH:, PATCH:]], 1),
            ],
            0,
        )

    def cut(field, row, by):
        strips = [field[h, pl.ds(row, PATCH), :] for h in range(halves)]
        return pltpu.roll(jnp.concatenate(strips, 1), by, 1)[:, :PATCH]

    def pairs(j, _):
        probe_re, probe_im = probe_ref[0], probe_ref[1]
        members = [PAIRS * j + u for u in range(PAIRS)]
        where, cuts, halves_in = [], [], []
        for i in members:
            waves = []
            for k in range(2):
                row = pos_ref[0, 2 * i + k] + RIM
                lane = pos_ref[1, 2 * i + k] + RIM
                back_by = (WIN - lane) & (WIN - 1)
                cos = cut(cosf, row, back_by)
                sin = cut(sinf, row, back_by)
                where.append((row, lane))
                cuts.append((cos, sin))
                wave_re = probe_re * cos - probe_im * sin
                wave_im = probe_re * sin + probe_im * cos
                waves.append(jnp.concatenate([wave_re, wave_im], 1))
            halves_in.append(jnp.concatenate(waves, 0))
        half = [regroup(right3(x, 0)) for x in halves_in]
        far = [left3(1, x) for x in half]
        weighted = []
        for i, x in zip(members, far):
            far_re, far_im = x[:PATCH], x[PATCH:]
            meas = jnp.concatenate([meas_ref[2 * i], meas_ref[2 * i + 1]], 1).astype(F32)
            weight = GRAD_SCALE * (far_re * far_re + far_im * far_im - meas)
            weighted.append(jnp.concatenate([weight * far_re, weight * far_im], 0))
        half = [regroup(left(0, x)) for x in weighted]
        back = [right(x, 1) for x in half]
        placed, rows_at = [], []
        for u in range(2 * PAIRS):
            row, lane = where[u]
            cos, sin = cuts[u]
            k = u % 2
            back_re = back[u // 2][k * PATCH : (k + 1) * PATCH, :PATCH]
            back_im = back[u // 2][k * PATCH : (k + 1) * PATCH, PATCH:]
            grad_re = probe_re * back_re + probe_im * back_im
            grad_im = probe_re * back_im - probe_im * back_re
            grad = cos * grad_im - sin * grad_re
            grad = jnp.concatenate([grad, jnp.zeros_like(grad)], 1)
            placed.append(pltpu.roll(grad, lane, 1).astype(BF16))
            rows_at.append(lax.broadcasted_iota(jnp.int32, (1, PATCH), 1) + row)
        row_at = jnp.concatenate(rows_at, 1)
        ext_row = lax.broadcasted_iota(jnp.int32, (slots * rows, row_at.shape[1]), 0)
        select = jnp.where(ext_row == row_at, 1.0, 0.0).astype(BF16)
        acc[...] = acc[...] + mm(select, jnp.concatenate(placed, 0))
        return 0

    lax.fori_loop(0, count // (2 * PAIRS), pairs, 0)

    grad_ref[...] = acc[...].astype(BF16).reshape(slots, rows, WIN)

    def b_edge_copy(k, other, source, owner):
        return pltpu.make_async_remote_copy(
            src_ref=grad_ref.at[source], dst_ref=grad_edge.at[col],
            send_sem=b_edge_send.at[k], recv_sem=b_edge_recv.at[col],
            device_id={"slab": slab, "strip": other * col_tiles + owner}, device_id_type=MESH,
        )

    def b_edge_copies(act):
        @pl.when(group > 0)
        def _():
            for k in range(edge):
                act(b_edge_copy(k, group - 1, k, col_tiles - edge + k))

        @pl.when(group < groups - 1)
        def _():
            for k in range(edge):
                act(b_edge_copy(edge + k, group + 1, edge + col_tiles + k, k))

    b_edge_copies(lambda copy: copy.start())
    b_group_copies = []
    for step in range(1, col_tiles):
        tile = lax.rem(col + step, col_tiles)
        copy = pltpu.make_async_remote_copy(
            src_ref=grad_ref.at[edge + tile], dst_ref=grad_land.at[step - 1],
            send_sem=b_send.at[step - 1], recv_sem=b_recv.at[step - 1],
            device_id={"slab": slab, "strip": group * col_tiles + tile}, device_id_type=MESH,
        )
        copy.start()
        b_group_copies.append(copy)
    total[...] = jnp.zeros((rows, wide), F32)

    total[:, window(col)] = total[:, window(col)] + grad_ref[edge + col].astype(F32)
    for step in range(1, col_tiles):
        b_group_copies[step - 1].wait_recv()
        at = window(lax.rem(col + col_tiles - step, col_tiles))
        total[:, at] = total[:, at] + grad_land[step - 1].astype(F32)

    has_edge = ((col < edge) & (group > 0)) | ((col >= col_tiles - edge) & (group < groups - 1))
    other = jnp.where(col < edge, group - 1, group + 1)

    @pl.when(has_edge)
    def _():
        for tile in range(col_tiles):
            pltpu.make_async_remote_copy(
                src_ref=grad_ref.at[0], dst_ref=grad_edge.at[tile],
                send_sem=b_edge_send.at[0], recv_sem=b_edge_recv.at[tile],
                device_id={"slab": slab, "strip": other * col_tiles + tile}, device_id_type=MESH,
            ).wait_recv()
            at = window(tile)
            total[:, at] = total[:, at] + grad_edge[tile].astype(F32)

    mine = jnp.where(inside, total[...], 0.0).astype(BF16)
    own[...] = mine
    b_copies = []
    for step in range(1, slabs):
        copy = pltpu.make_async_remote_copy(
            src_ref=own, dst_ref=grad_slab.at[step - 1],
            send_sem=b_slab_send.at[step - 1], recv_sem=b_slab_recv.at[step - 1],
            device_id={"slab": lax.rem(slab + step, slabs), "strip": strip}, device_id_type=MESH,
        )
        copy.start()
        b_copies.append(copy)

    out_ref[slab] = mine
    for step in range(1, slabs):
        b_copies[step - 1].wait_recv()
        out_ref[lax.rem(slab + slabs - step, slabs)] = grad_slab[step - 1]
    for copy in b_copies:
        copy.wait_send()
    for copy in b_group_copies:
        copy.wait_send()
    b_edge_copies(lambda copy: copy.wait_send())
    for copy in copies:
        copy.wait_send()
    for copy in group_copies:
        copy.wait_send()

    @pl.when(top | bottom)
    def _():
        for tile in range(col_tiles):
            edge_copy(tile).wait_send()


def spread_kernel(shear_ref, fields_ref, out_ref):
    depth, rows, width = out_ref.shape
    views, _, wide = fields_ref.shape
    for z in range(depth):
        result = jnp.zeros((rows, width), F32)
        for view in range(views):
            by = lax.rem(wide - RIM - shear_ref[view, z], wide)
            result = result + pltpu.roll(fields_ref[view].astype(F32), by, 1)[:, :width]
        out_ref[z] = result.astype(BF16)


def local(slabs, strips, volume, shear, probe, positions, measured):
    _, rows, width = volume.shape
    col_tiles = width // TILE_W
    wide = width + 2 * RIM
    edge = RIM // rows
    slots = col_tiles + 2 * edge
    others = max(slabs - 1, 1)
    vmem = pl.BlockSpec(memory_space=pltpu.VMEM)
    smem = pl.BlockSpec(memory_space=pltpu.SMEM)
    anywhere = pl.BlockSpec(memory_space=pl.ANY)
    dma = pltpu.SemaphoreType.DMA
    tables = jnp.asarray(dft_tables())
    patches = measured[0, 0]
    fields = pl.pallas_call(
        functools.partial(grad_kernel, slabs, strips),
        out_shape=jax.ShapeDtypeStruct((slabs, rows, wide), BF16),
        in_specs=[smem, smem, vmem, anywhere, anywhere, anywhere],
        out_specs=vmem,
        scratch_shapes=[
            pltpu.VMEM(probe.shape, F32),
            pltpu.VMEM(patches.shape, BF16),
            pltpu.VMEM(tables.shape, BF16),
            dma((3,)),
            pltpu.VMEM((others, rows, wide), BF16),
            pltpu.VMEM((others, rows, wide), BF16),
            pltpu.VMEM((rows, wide), BF16),
            pltpu.VMEM((col_tiles - 1, rows, WIN), BF16),
            pltpu.VMEM((2 * edge, rows, WIN), BF16),
            pltpu.VMEM((WIN // PATCH, slots * rows, PATCH), F32),
            pltpu.VMEM((WIN // PATCH, slots * rows, PATCH), F32),
            pltpu.VMEM((slots * rows, WIN), F32),
            pltpu.VMEM((slots, rows, WIN), BF16),
            pltpu.VMEM((col_tiles - 1, rows, WIN), BF16),
            pltpu.VMEM((col_tiles, rows, WIN), BF16),
            pltpu.VMEM((rows, wide), F32),
            pltpu.VMEM((rows, wide), BF16),
            pltpu.VMEM((others, rows, wide), BF16),
            dma((others,)), dma((others,)),
            dma((col_tiles - 1,)), dma((col_tiles - 1,)),
            dma((col_tiles,)), dma((2 * edge,)),
            dma((others,)), dma((others,)),
            dma((col_tiles - 1,)), dma((col_tiles - 1,)),
            dma((2 * edge,)), dma((col_tiles,)),
        ],
        compiler_params=pltpu.CompilerParams(collective_id=0, has_side_effects=True),
        name="gradient",
    )(shear, positions[0, 0].T, volume, probe, patches, tables)
    return pl.pallas_call(
        spread_kernel,
        out_shape=jax.ShapeDtypeStruct(volume.shape, BF16),
        in_specs=[smem, vmem],
        out_specs=vmem,
        name="spread",
    )(shear, fields)


def solution(mesh):
    placed = (
        P("slab", "strip", None),
        P(None, "slab"),
        P(),
        P("slab", "strip", None, None),
        P("slab", "strip", None, None, None),
    )
    return jax.shard_map(
        functools.partial(local, mesh.shape["slab"], mesh.shape["strip"]),
        mesh=mesh, in_specs=placed, out_specs=P("slab", "strip", None), check_vma=False,
    )
```

time: 34.7 us -> 28.7 us (0.83)
  Pallas kernels: 34.5 us -> 28.6 us
    pallas_call x3 -> x1, Pallas kernels: 32.5 us -> 26.6 us  [local(): pl.pallas_call(functools.partial(grad_kernel, slabs, strips), out_shape=j...]
where the time goes in v2:
time: 28.7 us; the launch traced here: 28.6 us
  Pallas kernels  28.6 us (100%)
    pallas_call x1, Pallas kernels, local(): pl.pallas_call(functools.partial(grad_kernel, slabs, strips), out_shape=j...  26.6 us
    pallas_call x1, Pallas kernels, local(): pl.pallas_call(spread_kernel, out_shape=jax.ShapeDtypeStruct(volume.shape...  2 us

profile of v2, /device:TPU:0, one launch (start us, length us, event | category | flops | bytes accessed | tf_op | source)
XLA Modules:
  0.0 28.6 jit_solution(17158733692430924407)
XLA Ops:
  0.0 26.6 %gradient.1.fields_ref = bf16[2,32,1152]{2,1,0:T(8,128)(2,1)} custom-call(s32[2,4]{1,0:T(2,128)} %shear_ref.3, s32[2,16]{1,0:T(2,128)} %bitcast.5, bf16[4,32,1024]{2,1,0:T(8,128)(2,1)} %vol_ref.1, f32[2,128,128]{2,1,0:T(8,128)} %probe_any.1, bf16[16,128,128]{2,1,0:T(8,128)(2,1)} %bitcast.4, bf16[4,256,256]{2,1,0:T(8,128)(2,1)} %constant.2.clone.tab_any), custom_call_target="tpu_custom_call" | custom-call | tf_op jit(solution)/shard_map/gradient/pallas_call | solution.py:420
  26.6 2.0 %spread.1 = bf16[4,32,1024]{2,1,0:T(8,128)(2,1)} custom-call(s32[2,4]{1,0:T(2,128)} %shear_ref.3, bf16[2,32,1152]{2,1,0:T(8,128)(2,1)} %gradient.1.fields_ref), custom_call_target="tpu_custom_call" | custom-call | tf_op jit(solution)/shard_map/spread/pallas_call | solution.py:454

commit v3 on v2

--- a/solution.py
+++ b/solution.py
@@ -14,7 +14,8 @@
 RIM = PATCH // 2
 WIN = TILE_W + 2 * RIM
 GRAD_SCALE = 0.125
-PAIRS = 4
+PAIRS = 8
+CUTS = 1
 MESH = pl.DeviceIdType.MESH
 F32 = jnp.float32
 BF16 = jnp.bfloat16
@@ -106,14 +107,16 @@
 
 
 def grad_kernel(
-    slabs, strips, shear_ref, pos_ref, vol_ref, probe_any, meas_any, tab_any, out_ref,
-    probe_ref, meas_ref, tab_ref, load_sem,
+    slabs, strips, shear_ref, pos_ref, vol_any, probe_any, meas_any, tab_any, out_ref,
+    vol_ref, probe_ref, meas_ref, tab_ref, load_sem,
     part, slab_in, proj, land, land_edge,
     cosf, sinf, acc, grad_ref, grad_land, grad_edge, total, own, grad_slab,
     slab_send, slab_recv, send, recv, edge_send, edge_recv,
     b_slab_send, b_slab_recv, b_send, b_recv, b_edge_send, b_edge_recv,
 ):
-    pairs_of = ((probe_any, probe_ref), (meas_any, meas_ref), (tab_any, tab_ref))
+    pairs_of = (
+        (vol_any, vol_ref), (probe_any, probe_ref), (meas_any, meas_ref), (tab_any, tab_ref),
+    )
     loads = [pltpu.make_async_copy(a, b, load_sem.at[k]) for k, (a, b) in enumerate(pairs_of)]
     for load in loads:
         load.start()
@@ -124,6 +127,8 @@
     edge = RIM // rows
     slots = col_tiles + 2 * edge
     halves = WIN // PATCH
+    cut_rows = rows // CUTS
+    cuts_at = [pl.ds(h * cut_rows, cut_rows) for h in range(CUTS)]
     slab, strip = place()
     group, col = strip // col_tiles, strip % col_tiles
     barrier, peers = greet(slab, strip, slabs, strips, col_tiles, edge)
@@ -148,26 +153,24 @@
             total = total + pltpu.roll(layer, shear_ref[view, z] + RIM, 1)
         return jnp.where(inside, total, 0.0).astype(BF16)
 
+    loads[0].wait()
     copies = []
     for step in range(1, slabs):
         view = lax.rem(slab + step, slabs)
         part[step - 1] = partial(view)
         if step == 1:
             pl.semaphore_wait(barrier, peers)
-        copy = pltpu.make_async_remote_copy(
-            src_ref=part.at[step - 1], dst_ref=slab_in.at[step - 1],
-            send_sem=slab_send.at[step - 1], recv_sem=slab_recv.at[step - 1],
-            device_id={"slab": view, "strip": strip}, device_id_type=MESH,
-        )
-        copy.start()
-        copies.append(copy)
+        for h, at in enumerate(cuts_at):
+            copy = pltpu.make_async_remote_copy(
+                src_ref=part.at[step - 1, at], dst_ref=slab_in.at[step - 1, at],
+                send_sem=slab_send.at[step - 1, h], recv_sem=slab_recv.at[step - 1, h],
+                device_id={"slab": view, "strip": strip}, device_id_type=MESH,
+            )
+            copy.start()
+            copies.append(copy)
     summed = partial(slab).astype(F32)
     if slabs == 1:
         pl.semaphore_wait(barrier, peers)
-    for step in range(1, slabs):
-        copies[step - 1].wait_recv()
-        summed = summed + slab_in[step - 1].astype(F32)
-    proj[...] = summed.astype(BF16)
 
     def window(tile):
         return pl.ds(pl.multiple_of(tile * TILE_W, TILE_W), WIN)
@@ -177,43 +180,59 @@
     other = jnp.where(col < edge, group - 1, group + 1)
     slot = jnp.where(col < edge, edge + col, col - (col_tiles - edge))
 
-    def edge_copy(tile):
+    def edge_copy(tile, h):
         return pltpu.make_async_remote_copy(
-            src_ref=proj.at[:, pl.ds(tile * TILE_W, WIN)], dst_ref=land_edge.at[slot],
-            send_sem=edge_send.at[tile], recv_sem=edge_recv.at[slot],
+            src_ref=proj.at[cuts_at[h], pl.ds(tile * TILE_W, WIN)],
+            dst_ref=land_edge.at[slot, cuts_at[h]],
+            send_sem=edge_send.at[tile, h], recv_sem=edge_recv.at[slot, h],
             device_id={"slab": slab, "strip": other * col_tiles + tile}, device_id_type=MESH,
         )
 
-    @pl.when(top | bottom)
-    def _():
-        for tile in range(col_tiles):
-            edge_copy(tile).start()
-
-    group_copies = []
-    for step in range(1, col_tiles):
-        tile = lax.rem(col + step, col_tiles)
-        copy = pltpu.make_async_remote_copy(
-            src_ref=proj.at[:, window(tile)], dst_ref=land.at[step - 1],
-            send_sem=send.at[step - 1], recv_sem=recv.at[step - 1],
-            device_id={"slab": slab, "strip": group * col_tiles + tile}, device_id_type=MESH,
-        )
-        copy.start()
-        group_copies.append(copy)
+    group_copies = [[] for _ in range(col_tiles)]
+
+    def send_windows(h):
+        @pl.when(top | bottom)
+        def _():
+            for tile in range(col_tiles):
+                edge_copy(tile, h).start()
+
+        for step in range(1, col_tiles):
+            tile = lax.rem(col + step, col_tiles)
+            copy = pltpu.make_async_remote_copy(
+                src_ref=proj.at[cuts_at[h], window(tile)],
+                dst_ref=land.at[step - 1, cuts_at[h]],
+                send_sem=send.at[step - 1, h], recv_sem=recv.at[step - 1, h],
+                device_id={"slab": slab, "strip": group * col_tiles + tile}, device_id_type=MESH,
+            )
+            copy.start()
+            group_copies[step].append(copy)
+
+    for h, at in enumerate(cuts_at):
+        value = summed[h * cut_rows : (h + 1) * cut_rows]
+        for step in range(1, slabs):
+            copies[CUTS * (step - 1) + h].wait_recv()
+            value = value + slab_in[step - 1, at].astype(F32)
+        proj[at] = value.astype(BF16)
+        send_windows(h)
     trig(edge + col, proj[:, window(col)])
     acc[...] = jnp.zeros_like(acc)
     for step in range(1, col_tiles):
-        group_copies[step - 1].wait_recv()
+        for copy in group_copies[step]:
+            copy.wait_recv()
         trig(edge + lax.rem(col + col_tiles - step, col_tiles), land[step - 1])
 
     def edge_in(first, place_at, has):
         @pl.when(has)
         def _():
             for k in range(edge):
-                pltpu.make_async_remote_copy(
-                    src_ref=proj.at[:, pl.ds(0, WIN)], dst_ref=land_edge.at[first + k],
-                    send_sem=edge_send.at[0], recv_sem=edge_recv.at[first + k],
-                    device_id={"slab": slab, "strip": other * col_tiles}, device_id_type=MESH,
-                ).wait_recv()
+                for h, at in enumerate(cuts_at):
+                    pltpu.make_async_remote_copy(
+                        src_ref=proj.at[at, pl.ds(0, WIN)],
+                        dst_ref=land_edge.at[first + k, at],
+                        send_sem=edge_send.at[0, h], recv_sem=edge_recv.at[first + k, h],
+                        device_id={"slab": slab, "strip": other * col_tiles},
+                        device_id_type=MESH,
+                    ).wait_recv()
                 trig(place_at + k, land_edge[first + k])
 
         @pl.when(jnp.logical_not(has))
@@ -226,7 +245,7 @@
     edge_in(0, 0, group > 0)
     edge_in(edge, edge + col_tiles, group < groups - 1)
 
-    for load in loads:
+    for load in loads[1:]:
         load.wait()
     count = meas_ref.shape[0]
 
@@ -310,87 +329,86 @@
 
     grad_ref[...] = acc[...].astype(BF16).reshape(slots, rows, WIN)
 
-    def b_edge_copy(k, other, source, owner):
+    def b_edge_copy(h, k, to_group, source, owner):
         return pltpu.make_async_remote_copy(
-            src_ref=grad_ref.at[source], dst_ref=grad_edge.at[col],
-            send_sem=b_edge_send.at[k], recv_sem=b_edge_recv.at[col],
-            device_id={"slab": slab, "strip": other * col_tiles + owner}, device_id_type=MESH,
+            src_ref=grad_ref.at[source, cuts_at[h]], dst_ref=grad_edge.at[col, cuts_at[h]],
+            send_sem=b_edge_send.at[k, h], recv_sem=b_edge_recv.at[col, h],
+            device_id={"slab": slab, "strip": to_group * col_tiles + owner}, device_id_type=MESH,
         )
 
-    def b_edge_copies(act):
+    def b_edge_copies(h, act):
         @pl.when(group > 0)
         def _():
             for k in range(edge):
-                act(b_edge_copy(k, group - 1, k, col_tiles - edge + k))
+                act(b_edge_copy(h, k, group - 1, k, col_tiles - edge + k))
 
         @pl.when(group < groups - 1)
         def _():
             for k in range(edge):
-                act(b_edge_copy(edge + k, group + 1, edge + col_tiles + k, k))
-
-    b_edge_copies(lambda copy: copy.start())
+                act(b_edge_copy(h, edge + k, group + 1, edge + col_tiles + k, k))
+
     b_group_copies = []
-    for step in range(1, col_tiles):
-        tile = lax.rem(col + step, col_tiles)
-        copy = pltpu.make_async_remote_copy(
-            src_ref=grad_ref.at[edge + tile], dst_ref=grad_land.at[step - 1],
-            send_sem=b_send.at[step - 1], recv_sem=b_recv.at[step - 1],
-            device_id={"slab": slab, "strip": group * col_tiles + tile}, device_id_type=MESH,
-        )
-        copy.start()
-        b_group_copies.append(copy)
+    for h, at in enumerate(cuts_at):
+        b_edge_copies(h, lambda copy: copy.start())
+        b_group_copies.append([])
+        for step in range(1, col_tiles):
+            tile = lax.rem(col + step, col_tiles)
+            copy = pltpu.make_async_remote_copy(
+                src_ref=grad_ref.at[edge + tile, at], dst_ref=grad_land.at[step - 1, at],
+                send_sem=b_send.at[step - 1, h], recv_sem=b_recv.at[step - 1, h],
+                device_id={"slab": slab, "strip": group * col_tiles + tile}, device_id_type=MESH,
+            )
+            copy.start()
+            b_group_copies[h].append(copy)
     total[...] = jnp.zeros((rows, wide), F32)
-
     total[:, window(col)] = total[:, window(col)] + grad_ref[edge + col].astype(F32)
-    for step in range(1, col_tiles):
-        b_group_copies[step - 1].wait_recv()
-        at = window(lax.rem(col + col_tiles - step, col_tiles))
-        total[:, at] = total[:, at] + grad_land[step - 1].astype(F32)
-
-    has_edge = ((col < edge) & (group > 0)) | ((col >= col_tiles - edge) & (group < groups - 1))
-    other = jnp.where(col < edge, group - 1, group + 1)
-
-    @pl.when(has_edge)
-    def _():
-        for tile in range(col_tiles):
-            pltpu.make_async_remote_copy(
-                src_ref=grad_ref.at[0], dst_ref=grad_edge.at[tile],
-                send_sem=b_edge_send.at[0], recv_sem=b_edge_recv.at[tile],
-                device_id={"slab": slab, "strip": other * col_tiles + tile}, device_id_type=MESH,
-            ).wait_recv()
-            at = window(tile)
-            total[:, at] = total[:, at] + grad_edge[tile].astype(F32)
-
-    mine = jnp.where(inside, total[...], 0.0).astype(BF16)
-    own[...] = mine
     b_copies = []
+    for h, at in enumerate(cuts_at):
+        for step in range(1, col_tiles):
+            b_group_copies[h][step - 1].wait_recv()
+            to = window(lax.rem(col + col_tiles - step, col_tiles))
+            total[at, to] = total[at, to] + grad_land[step - 1, at].astype(F32)
+
+        @pl.when(top | bottom)
+        def _():
+            for tile in range(col_tiles):
+                pltpu.make_async_remote_copy(
+                    src_ref=grad_ref.at[0, at], dst_ref=grad_edge.at[tile, at],
+                    send_sem=b_edge_send.at[0, h], recv_sem=b_edge_recv.at[tile, h],
+                    device_id={"slab": slab, "strip": other * col_tiles + tile},
+                    device_id_type=MESH,
+                ).wait_recv()
+                to = window(tile)
+                total[at, to] = total[at, to] + grad_edge[tile, at].astype(F32)
+
+        own[at] = jnp.where(inside[:cut_rows], total[at], 0.0).astype(BF16)
+        for step in range(1, slabs):
+            copy = pltpu.make_async_remote_copy(
+                src_ref=own.at[at], dst_ref=grad_slab.at[step - 1, at],
+                send_sem=b_slab_send.at[step - 1, h], recv_sem=b_slab_recv.at[step - 1, h],
+                device_id={"slab": lax.rem(slab + step, slabs), "strip": strip},
+                device_id_type=MESH,
+            )
+            copy.start()
+            b_copies.append(copy)
+
+    out_ref[slab] = own[...]
+    for copy in b_copies:
+        copy.wait_recv()
     for step in range(1, slabs):
-        copy = pltpu.make_async_remote_copy(
-            src_ref=own, dst_ref=grad_slab.at[step - 1],
-            send_sem=b_slab_send.at[step - 1], recv_sem=b_slab_recv.at[step - 1],
-            device_id={"slab": lax.rem(slab + step, slabs), "strip": strip}, device_id_type=MESH,
-        )
-        copy.start()
-        b_copies.append(copy)
-
-    out_ref[slab] = mine
-    for step in range(1, slabs):
-        b_copies[step - 1].wait_recv()
         out_ref[lax.rem(slab + slabs - step, slabs)] = grad_slab[step - 1]
-    for copy in b_copies:
+    for copy in b_copies + sum(b_group_copies, []):
         copy.wait_send()
-    for copy in b_group_copies:
-        copy.wait_send()
-    b_edge_copies(lambda copy: copy.wait_send())
-    for copy in copies:
-        copy.wait_send()
-    for copy in group_copies:
+    for h in range(CUTS):
+        b_edge_copies(h, lambda copy: copy.wait_send())
+    for copy in copies + sum(group_copies, []):
         copy.wait_send()
 
     @pl.when(top | bottom)
     def _():
         for tile in range(col_tiles):
-            edge_copy(tile).wait_send()
+            for h in range(CUTS):
+                edge_copy(tile, h).wait_send()
 
 
 def spread_kernel(shear_ref, fields_ref, out_ref):
@@ -420,13 +438,14 @@
     fields = pl.pallas_call(
         functools.partial(grad_kernel, slabs, strips),
         out_shape=jax.ShapeDtypeStruct((slabs, rows, wide), BF16),
-        in_specs=[smem, smem, vmem, anywhere, anywhere, anywhere],
+        in_specs=[smem, smem, anywhere, anywhere, anywhere, anywhere],
         out_specs=vmem,
         scratch_shapes=[
+            pltpu.VMEM(volume.shape, BF16),
             pltpu.VMEM(probe.shape, F32),
             pltpu.VMEM(patches.shape, BF16),
             pltpu.VMEM(tables.shape, BF16),
-            dma((3,)),
+            dma((4,)),
             pltpu.VMEM((others, rows, wide), BF16),
             pltpu.VMEM((others, rows, wide), BF16),
             pltpu.VMEM((rows, wide), BF16),
@@ -441,12 +460,12 @@
             pltpu.VMEM((rows, wide), F32),
             pltpu.VMEM((rows, wide), BF16),
             pltpu.VMEM((others, rows, wide), BF16),
-            dma((others,)), dma((others,)),
-            dma((col_tiles - 1,)), dma((col_tiles - 1,)),
-            dma((col_tiles,)), dma((2 * edge,)),
-            dma((others,)), dma((others,)),
-            dma((col_tiles - 1,)), dma((col_tiles - 1,)),
-            dma((2 * edge,)), dma((col_tiles,)),
+            dma((others, CUTS)), dma((others, CUTS)),
+            dma((col_tiles - 1, CUTS)), dma((col_tiles - 1, CUTS)),
+            dma((col_tiles, CUTS)), dma((2 * edge, CUTS)),
+            dma((others, CUTS)), dma((others, CUTS)),
+            dma((col_tiles - 1, CUTS)), dma((col_tiles - 1, CUTS)),
+            dma((2 * edge, CUTS)), dma((col_tiles, CUTS)),
         ],
         compiler_params=pltpu.CompilerParams(collective_id=0, has_side_effects=True),
         name="gradient",

time: 28.7 us -> 28 us (0.976)
  Pallas kernels: 28.6 us -> 27.8 us
    pallas_call x1, Pallas kernels: 26.6 us -> 25.8 us  [local(): pl.pallas_call(functools.partial(grad_kernel, slabs, strips), out_shape=j...]
where the time goes in v3:
time: 28 us; the launch traced here: 27.8 us
  Pallas kernels  27.8 us (99%)
    pallas_call x1, Pallas kernels, local(): pl.pallas_call(functools.partial(grad_kernel, slabs, strips), out_shape=j...  25.8 us
    pallas_call x1, Pallas kernels, local(): pl.pallas_call(spread_kernel, out_shape=jax.ShapeDtypeStruct(volume.shape...  2 us

profile of v3, /device:TPU:0, one launch (start us, length us, event | category | flops | bytes accessed | tf_op | source)
XLA Modules:
  0.0 27.8 jit_solution(4101113879965710801)
XLA Ops:
  0.0 25.8 %gradient.1.fields_ref = bf16[2,32,1152]{2,1,0:T(8,128)(2,1)} custom-call(s32[2,4]{1,0:T(2,128)} %shear_ref.3, s32[2,16]{1,0:T(2,128)} %bitcast.5, bf16[4,32,1024]{2,1,0:T(8,128)(2,1)} %vol_any.1, f32[2,128,128]{2,1,0:T(8,128)} %probe_any.1, bf16[16,128,128]{2,1,0:T(8,128)(2,1)} %bitcast.4, bf16[4,256,256]{2,1,0:T(8,128)(2,1)} %constant.2.clone.tab_any), custom_call_target="tpu_custom_call" | custom-call | tf_op jit(solution)/shard_map/gradient/pallas_call | solution.py:438
  25.8 2.0 %spread.1 = bf16[4,32,1024]{2,1,0:T(8,128)(2,1)} custom-call(s32[2,4]{1,0:T(2,128)} %shear_ref.3, bf16[2,32,1152]{2,1,0:T(8,128)(2,1)} %gradient.1.fields_ref), custom_call_target="tpu_custom_call" | custom-call | tf_op jit(solution)/shard_map/spread/pallas_call | solution.py:473
